TPU v7x, 32 devices: a whole 2x2x4 slice. The times are simulated.
32 devices in a mesh: dp: 8 (over z, x), tensor: 4 (over y, core).
Axes of the slice: x: 2, y: 2, z: 4, core: 2. Of those that a mesh axis runs over, the one named last changes fastest.
Arguments:
- tokens_in: bfloat16 [16384, 1152], P(('dp', 'tensor')), may hold values from -6 to 6
- condition: bfloat16 [16, 1152], P('dp'), may hold values from -6 to 6
- w_ada: bfloat16 [1152, 6912], P('dp', 'tensor'), may hold values from -0.1875 to 0.1875
- b_ada: bfloat16 [6912], P('tensor'), may hold values from -3 to 3
- w_qkv: bfloat16 [1152, 3456], P('dp', 'tensor'), may hold values from -0.1875 to 0.1875
- b_qv: bfloat16 [2304], P('tensor'), may hold values from -3 to 3
- w_proj: bfloat16 [1152, 1152], P('tensor', 'dp'), may hold values from -2 to 2
- b_proj: bfloat16 [1152], replicated, may hold values from -3 to 3
- w_fc1: bfloat16 [1152, 4608], P('dp', 'tensor'), may hold values from -0.1875 to 0.1875
- b_fc1: bfloat16 [4608], P('tensor'), may hold values from -3 to 3
- w_fc2: bfloat16 [4608, 1152], P('tensor', 'dp'), may hold values from -0.09375 to 0.09375
- b_fc2: bfloat16 [1152], replicated, may hold values from -3 to 3
- cotangent: bfloat16 [16384, 1152], P(('dp', 'tensor')), may hold values from -6 to 6
Outputs:
- block_out: bfloat16 [16384, 1152], P(('dp', 'tensor'))
- grad_tokens: float32 [16384, 1152], P(('dp', 'tensor'))
- grad_condition: float32 [16, 1152], P('dp')
- grad_w_ada: float32 [1152, 6912], P('dp', 'tensor')
- grad_b_ada: float32 [6912], P('tensor')
- grad_w_qkv: float32 [1152, 3456], P('dp', 'tensor')
- grad_b_qv: float32 [2304], P('tensor')
- grad_w_proj: float32 [1152, 1152], P('tensor', 'dp')
- grad_b_proj: float32 [1152], replicated
- grad_w_fc1: float32 [1152, 4608], P('dp', 'tensor')
- grad_b_fc1: float32 [4608], P('tensor')
- grad_w_fc2: float32 [4608, 1152], P('tensor', 'dp')
- grad_b_fc2: float32 [1152], replicated
All inputs are finite; a program needn't handle non-finite values.
Results may differ from a plain program's by a relative error of at most 0.015.
The roundings to bfloat16 on the way count: a program that leaves them out, or rounds other values in their place, can miss the bound.
Values may be sent and summed in bfloat16 or wider, within the bound.
No kernel may reach another device: no remote copies, remote signals or barrier semaphores. Data moves between devices by JAX's collectives and lax.ppermute only.
A program may use at most 192 MiB of HBM per device.

v0:
```python
import jax
import jax.numpy as jnp
from jax import lax
from jax.sharding import PartitionSpec as P

HEAD_DIM = 72
SEQ = 1024
highest = lax.Precision.HIGHEST
root_two_pi = 0.7978845608028654
cubic_term = 0.044715
epsilon = 1e-06


def normalize(values):
    centre = values - jnp.mean(values, axis=-1, keepdims=True)
    inverse = lax.rsqrt(jnp.mean(centre * centre, axis=-1, keepdims=True) + epsilon)
    return (centre * inverse, inverse)


def norm_back(normed, inverse, grad_in):
    mean_grad = jnp.mean(grad_in, axis=-1, keepdims=True)
    mean_cross = jnp.mean(grad_in * normed, axis=-1, keepdims=True)
    return inverse * (grad_in - mean_grad - normed * mean_cross)


def gelu_parts(pre_act):
    tangent = jnp.tanh(root_two_pi * (pre_act + cubic_term * pre_act * pre_act * pre_act))
    activated = 0.5 * pre_act * (1.0 + tangent)
    gelu_slope = 0.5 * (1.0 + tangent) + 0.5 * pre_act * (1.0 - tangent * tangent) * root_two_pi * (
        1.0 + 3.0 * cubic_term * pre_act * pre_act
    )
    return (activated, gelu_slope)


def fetch_weights(w_qkv, w_fc1, w_ada, w_proj, w_fc2):
    columns = (
        lax.all_gather(w_qkv, "dp", axis=0, tiled=True),
        lax.all_gather(w_fc1, "dp", axis=0, tiled=True),
        lax.all_gather(w_ada, "dp", axis=0, tiled=True),
    )
    row_parts = (
        lax.all_gather(w_proj, "dp", axis=1, tiled=True),
        lax.all_gather(w_fc2, "dp", axis=1, tiled=True),
    )
    return (columns, row_parts)


def gather_rows(values):
    return lax.all_gather(values, "tensor", axis=0, tiled=True)


def sum_back(row_term, row_count):
    return lax.psum_scatter(
        row_term(jnp.int32(0), lax.axis_size("tensor") * row_count).astype(jnp.bfloat16),
        "tensor",
        scatter_dimension=0,
        tiled=True,
    ).astype(jnp.float32)


def right_product(left_rows, right_mat):
    return jnp.dot(left_rows, right_mat, preferred_element_type=jnp.float32)


def transposed_product(left_rows, right_mat):

    def row_term(row_start, row_count):
        return lax.dot_general(
            left_rows, right_mat, (((1,), (1,)), ((), ())), preferred_element_type=jnp.float32
        )

    return row_term


def back_fold(weight_mat, kept_all, shard_rows):
    rows_in = lax.dot_general(
        shard_rows, weight_mat, (((1,), (1,)), ((), ())), preferred_element_type=jnp.float32
    )
    grad_weight = lax.dot_general(
        kept_all, shard_rows, (((0,), (0,)), ((), ())), preferred_element_type=jnp.float32
    )
    return (rows_in, grad_weight)


def attend(operands):
    queries, keys_b, values_b = operands
    score_scale = queries.shape[-1] ** (-0.5)
    scores = (
        jnp.einsum("qhd,khd->hqk", queries, keys_b, preferred_element_type=jnp.float32)
        * score_scale
    )
    row_max = jnp.max(scores, axis=-1, keepdims=True)
    exponent = jnp.exp(scores - row_max)
    row_total = jnp.sum(exponent, axis=-1, keepdims=True)
    attn_probs = (exponent / row_total).astype(jnp.bfloat16)
    mixture = jnp.einsum("hqk,khd->qhd", attn_probs, values_b, preferred_element_type=jnp.float32)
    return (mixture.astype(jnp.bfloat16), (row_max + jnp.log(row_total))[..., 0])


def attend_back(operands):
    queries, keys_b, values_b, grad_mix, logsum = operands
    score_scale = queries.shape[-1] ** (-0.5)
    scores = (
        jnp.einsum("qhd,khd->hqk", queries, keys_b, preferred_element_type=jnp.float32)
        * score_scale
    )
    attn_probs = jnp.exp(scores - logsum[..., None])
    grad_probs = jnp.einsum("qhd,khd->hqk", grad_mix, values_b, preferred_element_type=jnp.float32)
    row_inner = jnp.sum(grad_probs * attn_probs, axis=-1, keepdims=True)
    grad_scores = (attn_probs * (grad_probs - row_inner)).astype(jnp.bfloat16)
    grad_queries = (
        jnp.einsum("hqk,khd->qhd", grad_scores, keys_b, preferred_element_type=jnp.float32)
        * score_scale
    )
    grad_keys = (
        jnp.einsum("hqk,qhd->khd", grad_scores, queries, preferred_element_type=jnp.float32)
        * score_scale
    )
    grad_values = jnp.einsum(
        "hqk,qhd->khd",
        attn_probs.astype(jnp.bfloat16),
        grad_mix,
        preferred_element_type=jnp.float32,
    )
    return jnp.stack([grad_queries, grad_keys, grad_values], axis=2).astype(jnp.bfloat16)


def shards(
    tokens_in,
    condition,
    w_ada,
    b_ada,
    w_qkv,
    b_qv,
    w_proj,
    b_proj,
    w_fc1,
    b_fc1,
    w_fc2,
    b_fc2,
    cotangent,
):
    tok_rows = tokens_in.shape[0]
    latents = condition.shape[0]
    head_size = HEAD_DIM
    (qkv_full, fc1_full, ada_full), (proj_full, fc2_full) = fetch_weights(
        w_qkv, w_fc1, w_ada, w_proj, w_fc2
    )
    cond_vals = condition.astype(jnp.float32)
    cond_sigmoid = jax.nn.sigmoid(cond_vals)
    silu_cond = (cond_vals * cond_sigmoid).astype(jnp.bfloat16)
    mod_part = jnp.dot(silu_cond, ada_full, preferred_element_type=jnp.float32) + b_ada.astype(
        jnp.float32
    )
    modulation = lax.all_gather(mod_part, "tensor", axis=1, tiled=True)
    row_place = lax.axis_index("tensor") * tok_rows + jnp.arange(tok_rows, dtype=jnp.int32)
    onehot = (row_place[:, None] // SEQ == jnp.arange(latents, dtype=jnp.int32)[None, :]).astype(
        jnp.float32
    )
    mod_rows = jnp.dot(onehot, modulation, precision=highest)
    shift_attn, scale_attn, gate_attn, shift_mlp, scale_mlp, gate_mlp = jnp.split(
        mod_rows, 6, axis=1
    )
    input_vals = tokens_in.astype(jnp.float32)
    normed_one, inverse_one = normalize(input_vals)
    attn_in = (normed_one * (1.0 + scale_attn) + shift_attn).astype(jnp.bfloat16)
    attn_rows = gather_rows(attn_in)
    full_rows = attn_rows.shape[0]
    head_count = qkv_full.shape[1] // (3 * head_size)
    projected = jnp.dot(attn_rows, qkv_full, preferred_element_type=jnp.float32).reshape(
        full_rows, head_count, 3, head_size
    )
    bias_qv = b_qv.astype(jnp.float32).reshape(head_count, 2, head_size)
    block_shape = (full_rows // SEQ, SEQ, head_count, head_size)
    queries = (projected[:, :, 0] + bias_qv[:, 0]).astype(jnp.bfloat16).reshape(block_shape)
    keys_b = projected[:, :, 1].astype(jnp.bfloat16).reshape(block_shape)
    values_b = (projected[:, :, 2] + bias_qv[:, 1]).astype(jnp.bfloat16).reshape(block_shape)
    mixture, logsum = lax.map(attend, (queries, keys_b, values_b))
    mix_rows = mixture.reshape(full_rows, head_count * head_size)
    attn_out = lax.psum_scatter(
        right_product(mix_rows, proj_full).astype(jnp.bfloat16),
        "tensor",
        scatter_dimension=0,
        tiled=True,
    ).astype(jnp.float32) + b_proj.astype(jnp.float32)
    middle = input_vals + gate_attn * attn_out
    normed_two, inverse_two = normalize(middle)
    mlp_in = (normed_two * (1.0 + scale_mlp) + shift_mlp).astype(jnp.bfloat16)
    mlp_rows = gather_rows(mlp_in)
    pre_act = jnp.dot(mlp_rows, fc1_full, preferred_element_type=jnp.float32) + b_fc1.astype(
        jnp.float32
    )
    activated, gelu_slope = gelu_parts(pre_act)
    act_rows = activated.astype(jnp.bfloat16)
    mlp_out = lax.psum_scatter(
        right_product(act_rows, fc2_full).astype(jnp.bfloat16),
        "tensor",
        scatter_dimension=0,
        tiled=True,
    ).astype(jnp.float32) + b_fc2.astype(jnp.float32)
    result = middle + gate_mlp * mlp_out
    grad_out = cotangent.astype(jnp.float32)
    grad_mlp = (gate_mlp * grad_out).astype(jnp.bfloat16)
    d_gate_mlp = grad_out * mlp_out
    held_weights = lax.optimization_barrier((w_qkv, w_fc1, w_ada, w_proj, w_fc2, grad_mlp))
    (qkv_back, fc1_back, ada_back), (proj_back, fc2_back) = fetch_weights(
        held_weights[0], held_weights[1], held_weights[2], held_weights[3], held_weights[4]
    )
    grad_act, grad_fc2 = back_fold(
        fc2_back, act_rows, lax.all_gather(grad_mlp, "tensor", axis=0, tiled=True)
    )
    grad_pre = (grad_act * gelu_slope).astype(jnp.bfloat16)
    grad_fc1 = lax.dot_general(
        mlp_rows, grad_pre, (((0,), (0,)), ((), ())), preferred_element_type=jnp.float32
    )
    grad_mlp_in = sum_back(transposed_product(grad_pre, fc1_back), tok_rows)
    d_scale_mlp = grad_mlp_in * normed_two
    grad_middle = grad_out + norm_back(normed_two, inverse_two, grad_mlp_in * (1.0 + scale_mlp))
    grad_attn = (gate_attn * grad_middle).astype(jnp.bfloat16)
    d_gate_attn = grad_middle * attn_out
    grad_mixture, grad_proj = back_fold(
        proj_back, mix_rows, lax.all_gather(grad_attn, "tensor", axis=0, tiled=True)
    )
    grad_mix_b = grad_mixture.astype(jnp.bfloat16).reshape(block_shape)
    grad_qkv = lax.map(attend_back, (queries, keys_b, values_b, grad_mix_b, logsum)).reshape(
        full_rows, head_count * 3 * head_size
    )
    grad_wqkv = lax.dot_general(
        attn_rows, grad_qkv, (((0,), (0,)), ((), ())), preferred_element_type=jnp.float32
    )
    grad_attn_in = sum_back(transposed_product(grad_qkv, qkv_back), tok_rows)
    d_scale_attn = grad_attn_in * normed_one
    grad_tokens = grad_middle + norm_back(
        normed_one, inverse_one, grad_attn_in * (1.0 + scale_attn)
    )
    grad_mod_rows = jnp.concatenate(
        [grad_attn_in, d_scale_attn, d_gate_attn, grad_mlp_in, d_scale_mlp, d_gate_mlp], axis=1
    )
    grad_mod_all = jnp.dot(onehot.T, grad_mod_rows, precision=highest)
    grad_mod = lax.psum_scatter(
        grad_mod_all.astype(jnp.bfloat16), "tensor", scatter_dimension=1, tiled=True
    ).astype(jnp.float32)
    grad_ada = jnp.dot(silu_cond.astype(jnp.float32).T, grad_mod, precision=highest)
    grad_silu = jnp.dot(grad_mod, ada_back.T, precision=highest)
    grad_cond_part = grad_silu * cond_sigmoid * (1.0 + cond_vals * (1.0 - cond_sigmoid))
    qkv_sums = jnp.sum(
        grad_qkv.astype(jnp.float32).reshape(full_rows, head_count, 3, head_size), axis=0
    )
    grad_bqv_part = jnp.stack([qkv_sums[:, 0], qkv_sums[:, 2]], axis=1).reshape(-1)
    grad_b1_part = jnp.sum(grad_pre.astype(jnp.float32), axis=0)
    grad_bo_part = jnp.sum(grad_attn.astype(jnp.float32), axis=0)
    grad_b2_part = jnp.sum(grad_mlp.astype(jnp.float32), axis=0)
    grad_ba_part = jnp.sum(grad_mod, axis=0)
    grad_condition, grad_bo_mid, grad_b2_mid = lax.psum(
        (grad_cond_part, grad_bo_part, grad_b2_part), "tensor"
    )
    grad_bqv, grad_b1, grad_ba, grad_bo, grad_b2 = lax.psum(
        (grad_bqv_part, grad_b1_part, grad_ba_part, grad_bo_mid, grad_b2_mid), "dp"
    )
    owned_qkv, owned_fc1, owned_ada = (
        lax.psum_scatter(grad_wqkv, "dp", scatter_dimension=0, tiled=True),
        lax.psum_scatter(grad_fc1, "dp", scatter_dimension=0, tiled=True),
        lax.psum_scatter(grad_ada, "dp", scatter_dimension=0, tiled=True),
    )
    owned_proj, owned_fc2 = (
        lax.psum_scatter(grad_proj, "dp", scatter_dimension=1, tiled=True),
        lax.psum_scatter(grad_fc2, "dp", scatter_dimension=1, tiled=True),
    )
    return (
        result.astype(jnp.bfloat16),
        grad_tokens,
        grad_condition,
        owned_ada,
        grad_ba,
        owned_qkv,
        grad_bqv,
        owned_proj,
        grad_bo,
        owned_fc1,
        grad_b1,
        owned_fc2,
        grad_b2,
    )


def solution(mesh):
    placed = (
        P(("dp", "tensor"), None),
        P("dp", None),
        P("dp", "tensor"),
        P("tensor"),
        P("dp", "tensor"),
        P("tensor"),
        P("tensor", "dp"),
        P(),
        P("dp", "tensor"),
        P("tensor"),
        P("tensor", "dp"),
        P(),
        P(("dp", "tensor"), None),
    )
    return jax.shard_map(
        shards,
        mesh=mesh,
        in_specs=placed,
        out_specs=(
            P(("dp", "tensor"), None),
            P(("dp", "tensor"), None),
            P("dp", None),
            P("dp", "tensor"),
            P("tensor"),
            P("dp", "tensor"),
            P("tensor"),
            P("tensor", "dp"),
            P(),
            P("dp", "tensor"),
            P("tensor"),
            P("tensor", "dp"),
            P(),
        ),
        check_vma=False,
    )
```

profile of v0, /device:TPU:0, one launch (start us, length us, event | category | flops | bytes accessed | tf_op | source)
XLA Modules:
  0.0 1585.1 jit_solution(13999615193881543100)
XLA Ops:
  11.4 74.1 %all-gather.14.cloned.1.call-done = bf16[1152,1728]{1,0:T(8,128)(2,1)} async-done(((bf16[144,1728]{1,0:T(8,128)(2,1)}), bf16[1152,1728]{1,0:T(8,128)(2,1)}) %all-gather.14.cloned.1.call-update) | async-done | bytes 3981328 | tf_op jit(solution)/shard_map/all_gather | solution.py:39
  106.3 36.6 %all_gather.49 = bf16[288,1152]{0,1:T(8,128)(2,1)} all-gather(bf16[288,144]{0,1:T(8,128)(2,1)S(1)} %copy-done.24), channel_id=1, replica_groups=mesh['dp'=8,'tensor'=4] {'dp'}, dimensions={1}, use_global_device_ids=true | all-gather | bytes 746496 | tf_op jit(solution)/shard_map/all_gather | solution.py:42
  147.1 39.3 %all-gather.16.cloned.1.call-done = bf16[2048,1152]{1,0:T(8,128)(2,1)} async-done(((bf16[512,1152]{1,0:T(8,128)(2,1)}), bf16[2048,1152]{1,0:T(8,128)(2,1)}) %all-gather.16.cloned.1.call-update) | async-done | bytes 4718608 | tf_op jit(solution)/shard_map/all_gather | solution.py:49
  215.9 51.3 %while.22 = (s32[]{:T(128)}, bf16[2,1024,4,72]{1,3,2,0:T(8,128)(2,1)}, f32[2,4,1024]{2,1,0:T(4,128)S(1)}, bf16[2,1024,4,72]{1,3,2,0:T(8,128)(2,1)}, bf16[2,1024,...) while((s32[]{:T(128)}, bf16[2,1024,4,72]{1,3,2,0:T(8,128)(2,1)}, ...), condition=%wide.region_5.6_spmd, body=%wide.region_2.5_spmd.sunk | while | flops 1245999104 | bytes 66980012 | solution.py:178
  276.6 47.1 %reduce-scatter.13.cloned.1.call-done = bf16[512,1152]{1,0:T(8,128)(2,1)} async-done(((bf16[2048,1152]{1,0:T(8,128)(2,1)}), bf16[512,1152]{1,0:T(8,128)(2,1)}) %reduce-scatter.13.cloned.1.call-update) | async-done | bytes 1179664 | tf_op jit(solution)/shard_map/reduce_scatter | solution.py:180
  337.3 43.7 %all-gather.22.cloned.1.call-done = bf16[1152,1152]{1,0:T(8,128)(2,1)} async-done(((bf16[144,1152]{1,0:T(8,128)(2,1)}), bf16[1152,1152]{1,0:T(8,128)(2,1)}) %all-gather.22.cloned.1.call-update) | async-done | bytes 2654224 | tf_op jit(solution)/shard_map/all_gather | solution.py:38
  381.0 38.1 %all-gather.20.cloned.1.call-done = bf16[2048,1152]{1,0:T(8,128)(2,1)} async-done(((bf16[512,1152]{1,0:T(8,128)(2,1)}), bf16[2048,1152]{1,0:T(8,128)(2,1)}) %all-gather.20.cloned.1.call-update) | async-done | bytes 4718608 | tf_op jit(solution)/shard_map/all_gather | solution.py:49
  430.7 45.9 %all-gather.28.cloned.1.call-done = bf16[1152,1152]{0,1:T(8,128)(2,1)} async-done(((bf16[1152,144]{0,1:T(8,128)(2,1)}), bf16[1152,1152]{0,1:T(8,128)(2,1)}) %all-gather.28.cloned.1.call-update) | async-done | bytes 2654224 | tf_op jit(solution)/shard_map/all_gather | solution.py:43
  476.6 38.3 %all-gather.26.cloned.1.call-done = bf16[2048,1152]{1,0:T(8,128)(2,1)} async-done(((bf16[512,1152]{1,0:T(8,128)(2,1)}), bf16[2048,1152]{1,0:T(8,128)(2,1)}) %all-gather.26.cloned.1.call-update) | async-done | bytes 4718608 | tf_op jit(solution)/shard_map/all_gather | solution.py:210
  514.9 16.0 %convert_reduce_fusion = (f32[1152]{0:T(1024)}, bf16[2048,1152]{1,0:T(8,128)(2,1)}) fusion(f32[2048,1152]{1,0:T(8,128)} %convolution_add_fusion, bf16[2048,1152]{1,0:T(8,128)(2,1)} %all-gather.26.cloned.1.call-done, bf16[1152,1152]{0,1:T(8,128)(2,1)} %all-gather.28.cloned.1.call-done), kind=kOutput, calls=%fused_computation.64 | convolution fusion | flops 5485362176 | bytes 21533184 | tf_op jit(solution)/shard_map/dot_general | solution.py:76
  530.9 41.5 %all-gather.30.cloned.1.call-done = bf16[1152,1152]{1,0:T(8,128)(2,1)} async-done(((bf16[144,1152]{1,0:T(8,128)(2,1)}), bf16[1152,1152]{1,0:T(8,128)(2,1)}) %all-gather.30.cloned.1.call-update) | async-done | bytes 2654224 | tf_op jit(solution)/shard_map/all_gather | solution.py:38
  583.8 44.4 %all-gather.24.cloned.1.call-done = bf16[1152,1152]{0,1:T(8,128)(2,1)} async-done(((bf16[1152,144]{0,1:T(8,128)(2,1)}), bf16[1152,1152]{0,1:T(8,128)(2,1)}) %all-gather.24.cloned.1.call-update) | async-done | bytes 2654224 | tf_op jit(solution)/shard_map/all_gather | solution.py:43
  642.0 35.4 %reduce-scatter.17.cloned.1.call-done = bf16[512,1152]{1,0:T(8,128)(2,1)} async-done(((bf16[2048,1152]{1,0:T(8,128)(2,1)}), bf16[512,1152]{1,0:T(8,128)(2,1)}) %reduce-scatter.17.cloned.1.call-update) | async-done | bytes 1179664 | tf_op jit(solution)/shard_map/reduce_scatter | solution.py:53
  680.9 46.8 %reduce-scatter.15.cloned.1.call-done = bf16[512,1152]{1,0:T(8,128)(2,1)} async-done(((bf16[2048,1152]{1,0:T(8,128)(2,1)}), bf16[512,1152]{1,0:T(8,128)(2,1)}) %reduce-scatter.15.cloned.1.call-update) | async-done | bytes 1179664 | tf_op jit(solution)/shard_map/reduce_scatter | solution.py:195
  735.6 32.4 %all_gather.57 = bf16[288,1152]{0,1:T(8,128)(2,1)S(1)} all-gather(bf16[288,144]{0,1:T(8,128)(2,1)S(1)} %copy-done.25), channel_id=1, replica_groups=mesh['dp'=8,'tensor'=4] {'dp'}, dimensions={1}, use_global_device_ids=true | all-gather | bytes 746496 | tf_op jit(solution)/shard_map/all_gather | solution.py:42
  785.1 75.6 %while.23 = (s32[]{:T(128)}, bf16[2,1024,4,3,72]{1,4,2,3,0:T(8,128)(2,1)}, bf16[2,1024,4,72]{1,3,2,0:T(8,128)(2,1)S(1)}, bf16[2,1024,4,72]{1,3,2,0:T(8,128)(2,1)...) while((s32[]{:T(128)}, ...), condition=%wide.region_15.16_spmd, body=%wide.region_13.15_spmd.sunk | while | flops 3077009408 | bytes 199608528 | solution.py:225
  877.8 48.1 %reduce-scatter.19.cloned.1.call-done = bf16[512,1152]{1,0:T(8,128)(2,1)} async-done(((bf16[2048,1152]{1,0:T(8,128)(2,1)}), bf16[512,1152]{1,0:T(8,128)(2,1)}) %reduce-scatter.19.cloned.1.call-update) | async-done | bytes 1179664 | tf_op jit(solution)/shard_map/reduce_scatter | solution.py:53
  1000.2 49.2 %all-gather.36.cloned.1.call-done = bf16[1152,1728]{1,0:T(8,128)(2,1)} async-done(((bf16[144,1728]{1,0:T(8,128)(2,1)}), bf16[1152,1728]{1,0:T(8,128)(2,1)}) %all-gather.36.cloned.1.call-update) | async-done | bytes 3981328 | tf_op jit(solution)/shard_map/all_gather | solution.py:39
  1063.8 39.3 %all-reduce = (f32[1728]{0:T(1024)}, f32[576]{0:T(1024)}, f32[1152]{0:T(1024)}, f32[1152]{0:T(1024)}, f32[1152]{0:T(1024)}) all-reduce(f32[1728]{0:T(1024)S(1)} %convert_reduce_fusion.5, f32[576]{0:T(1024)S(1)} %reshape.219, f32[1152]{0:T(1024)S(1)} %get-tuple-element.178, ...), channel_id=1, replica_groups=mesh['dp'=8,'tensor'=4] {'dp'}, use_global_device_ids=true, to_apply=%region_23.24 | all-reduce | flops 5760 | bytes 46080 | tf_op jit(solution)/shard_map/psum | solution.py:257
  1103.1 54.5 %reduce-scatter.29.cloned.1.call-done = f32[1152,144]{0,1:T(8,128)} async-done(((f32[1152,1152]{0,1:T(8,128)}), f32[1152,144]{0,1:T(8,128)}) %reduce-scatter.29.cloned.1.call-update) | async-done | bytes 663568 | tf_op jit(solution)/shard_map/reduce_scatter | solution.py:267
  1157.7 108.1 %reduce-scatter.27.cloned.1.call-done = f32[144,1152]{1,0:T(8,128)} async-done(((f32[1152,1152]{1,0:T(8,128)}), f32[144,1152]{1,0:T(8,128)}) %reduce-scatter.27.cloned.1.call-update) | async-done | bytes 663568 | tf_op jit(solution)/shard_map/reduce_scatter | solution.py:262
  1265.8 70.3 %reduce-scatter.25.cloned.1.call-done = f32[288,144]{0,1:T(8,128)} async-done(((f32[288,1152]{0,1:T(8,128)}), f32[288,144]{0,1:T(8,128)}) %reduce-scatter.25.cloned.1.call-update) | async-done | bytes 165904 | tf_op jit(solution)/shard_map/reduce_scatter | solution.py:266
  1336.1 90.6 %reduce-scatter.23.cloned.1.call-done = f32[144,864]{1,0:T(8,128)} async-done(((f32[1152,864]{1,0:T(8,128)}), f32[144,864]{1,0:T(8,128)}) %reduce-scatter.23.cloned.1.call-update) | async-done | bytes 497680 | tf_op jit(solution)/shard_map/reduce_scatter | solution.py:261
  1426.7 151.3 %reduce-scatter.21.cloned.1.call-done = f32[144,1728]{1,0:T(8,128)} async-done(((f32[1152,1728]{1,0:T(8,128)}), f32[144,1728]{1,0:T(8,128)}) %reduce-scatter.21.cloned.1.call-update) | async-done | bytes 995344 | tf_op jit(solution)/shard_map/reduce_scatter | solution.py:263
  (262 shorter events, 378.2 us)
Async XLA Ops:
  7.2 78.3 %all-gather.14.cloned.1.call-start = ((), (), s32[]{:S(2)}) async-start(), calls=%async_computation.10 | async-start | bytes 4644864 | tf_op jit(solution)/shard_map/all_gather | solution.py:39
  7.9 139.1 %all-gather.18.cloned.1.call-start = ((), (), s32[]{:S(2)}) async-start(), calls=%async_computation.12 | async-start | bytes 2322432 | tf_op jit(solution)/shard_map/all_gather | solution.py:37
  8.7 177.7 %all-gather.16.cloned.1.call-start = ((), (), s32[]{:S(2)}) async-start(), calls=%async_computation.11 | async-start | bytes 5898240 | tf_op jit(solution)/shard_map/all_gather | solution.py:49
  106.1 217.6 %reduce-scatter.13.cloned.1.call-start = ((), (), s32[]{:S(2)}) async-start(), calls=%async_computation.13 | async-start | bytes 5898240 | tf_op jit(solution)/shard_map/reduce_scatter | solution.py:180
  275.7 105.3 %all-gather.22.cloned.1.call-start = ((), (), s32[]{:S(2)}) async-start(), calls=%async_computation.15 | async-start | bytes 2985984 | tf_op jit(solution)/shard_map/all_gather | solution.py:38
  276.3 142.9 %all-gather.20.cloned.1.call-start = ((), (), s32[]{:S(2)}) async-start(), calls=%async_computation.14 | async-start | bytes 5898240 | tf_op jit(solution)/shard_map/all_gather | solution.py:49
  326.6 401.0 %copy-start.33 = (f32[512]{0:T(512)}, f32[512]{0:T(512)S(1)}, u32[]{:S(2)}) copy-start(f32[512]{0:T(512)S(1)} %broadcast_multiply_fusion.4) | copy-start | bytes 6148
  328.7 398.9 %copy-start.37 = (f32[512]{0:T(512)}, f32[512]{0:T(512)S(1)}, u32[]{:S(2)}) copy-start(f32[512]{0:T(512)S(1)} %add_rsqrt_fusion) | copy-start | bytes 6148
  334.4 142.2 %all-gather.28.cloned.1.call-start = ((), (), s32[]{:S(2)}) async-start(), calls=%async_computation.19 | async-start | bytes 2985984 | tf_op jit(solution)/shard_map/all_gather | solution.py:43
  335.1 179.8 %all-gather.26.cloned.1.call-start = ((), (), s32[]{:S(2)}) async-start(), calls=%async_computation.18 | async-start | bytes 5898240 | tf_op jit(solution)/shard_map/all_gather | solution.py:210
  335.9 236.5 %all-gather.30.cloned.1.call-start = ((), (), s32[]{:S(2)}) async-start(), calls=%async_computation.20 | async-start | bytes 2985984 | tf_op jit(solution)/shard_map/all_gather | solution.py:38
  336.6 291.6 %all-gather.24.cloned.1.call-start = ((), (), s32[]{:S(2)}) async-start(), calls=%async_computation.16 | async-start | bytes 2985984 | tf_op jit(solution)/shard_map/all_gather | solution.py:43
  337.2 340.2 %reduce-scatter.17.cloned.1.call-start = ((), (), s32[]{:S(2)}) async-start(), calls=%async_computation.21 | async-start | bytes 5898240 | tf_op jit(solution)/shard_map/reduce_scatter | solution.py:53
  583.3 144.3 %reduce-scatter.15.cloned.1.call-start = ((), (), s32[]{:S(2)}) async-start(), calls=%async_computation.17 | async-start | bytes 5898240 | tf_op jit(solution)/shard_map/reduce_scatter | solution.py:195
  641.3 131.9 %all-gather.32.cloned.1.call-start = ((), (), s32[]{:S(2)}) async-start(), calls=%async_computation.22 | async-start | bytes 5898240 | tf_op jit(solution)/shard_map/all_gather | solution.py:222
  735.6 132.1 %all-gather.34.cloned.1.call-start = ((), (), s32[]{:S(2)}) async-start(), calls=%async_computation.23 | async-start | bytes 2322432 | tf_op jit(solution)/shard_map/all_gather | solution.py:37
  768.1 157.8 %reduce-scatter.19.cloned.1.call-start = ((), (), s32[]{:S(2)}) async-start(), calls=%async_computation.24 | async-start | bytes 5898240 | tf_op jit(solution)/shard_map/reduce_scatter | solution.py:53
  877.8 112.3 %reduce-scatter.31.cloned.1.call-start = ((), (), s32[]{:S(2)}) async-start(), calls=%async_computation.31 | async-start | bytes 2211840
  945.0 104.4 %all-gather.36.cloned.1.call-start = ((), (), s32[]{:S(2)}) async-start(), calls=%async_computation.25 | async-start | bytes 4644864 | tf_op jit(solution)/shard_map/all_gather | solution.py:39
  945.6 212.1 %reduce-scatter.29.cloned.1.call-start = ((), (), s32[]{:S(2)}) async-start(), calls=%async_computation.30 | async-start | bytes 5971968 | tf_op jit(solution)/shard_map/reduce_scatter | solution.py:267
  960.3 305.5 %reduce-scatter.27.cloned.1.call-start = ((), (), s32[]{:S(2)}) async-start(), calls=%async_computation.29 | async-start | bytes 5971968 | tf_op jit(solution)/shard_map/reduce_scatter | solution.py:262
  973.3 362.8 %reduce-scatter.25.cloned.1.call-start = ((), (), s32[]{:S(2)}) async-start(), calls=%async_computation.28 | async-start | bytes 1990656 | tf_op jit(solution)/shard_map/reduce_scatter | solution.py:266
  980.2 446.5 %reduce-scatter.23.cloned.1.call-start = ((), (), s32[]{:S(2)}) async-start(), calls=%async_computation.27 | async-start | bytes 4644864 | tf_op jit(solution)/shard_map/reduce_scatter | solution.py:261
  990.0 588.0 %reduce-scatter.21.cloned.1.call-start = ((), (), s32[]{:S(2)}) async-start(), calls=%async_computation.26 | async-start | bytes 9289728 | tf_op jit(solution)/shard_map/reduce_scatter | solution.py:263
  (55 other events, 958.5 us)
Sparse Core Ops, SparseCore 0:
  10.2 75.2 all-gather.13
  87.7 59.3 all-gather.17
  149.2 37.1 all-gather.15
  275.8 47.8 reduce-scatter.12
  326.0 55.0 all-gather.21
  383.1 36.0 all-gather.19
  421.5 55.0 all-gather.27
  478.8 36.0 all-gather.25
  517.3 55.0 all-gather.29
  574.6 53.5 all-gather.23
  630.9 46.3 reduce-scatter.16
  679.8 47.8 reduce-scatter.14
  735.7 37.4 all-gather.31
  775.5 48.9 all-gather.33
  877.9 47.9 reduce-scatter.18
  945.1 29.3 reduce-scatter.30
  976.8 72.5 all-gather.35
  1053.9 103.7 reduce-scatter.28
  1161.8 103.9 reduce-scatter.26
  1270.1 65.9 reduce-scatter.24
  1340.3 86.3 reduce-scatter.22
  1431.4 146.5 reduce-scatter.20
where the time goes:
time: 1590 us
  waiting for transfers between devices  1080 us (68%)
  matrix products  225 us (14%)
  blocking collectives  124 us (8%)
  other arithmetic  71.7 us (5%)
  local copies, waits for them, and re-layouts  64.6 us (4%)
    reduce_scatter x1, waiting for transfers between devices, shards(): lax.psum_scatter(grad_ada, 'dp', scatter_dimension=0, tiled=True)  151 us
    all_gather x2, waiting for transfers between devices, fetch_weights(): lax.all_gather(w_ada, 'dp', axis=0, tiled=True)  123 us
    reduce_scatter x1, waiting for transfers between devices, shards(): lax.psum_scatter(grad_fc1, 'dp', scatter_dimension=0, tiled=True)  108 us
    reduce_scatter x1, waiting for transfers between devices, shards(): lax.psum_scatter(grad_wqkv, 'dp', scatter_dimension=0, tiled=True)  90.6 us
    all_gather x2, waiting for transfers between devices, fetch_weights(): lax.all_gather(w_fc2, 'dp', axis=1, tiled=True)  90.3 us
    all_gather x2, waiting for transfers between devices, fetch_weights(): lax.all_gather(w_fc1, 'dp', axis=0, tiled=True)  85.2 us
    reduce_scatter x2, waiting for transfers between devices, sum_back(): lax.psum_scatter(row_term(jnp.int32(0), lax.axis_size('tensor') * row_cou...  83.5 us
    all_gather x2, waiting for transfers between devices, gather_rows(): return lax.all_gather(values, 'tensor', axis=0, tiled=True)  77.4 us
  transfers between devices with their start and end apart: 22, of which 20 were waited for; matrix products, arithmetic and copies ran while one was open for 14% of the time, Pallas kernels for 0%

commit v1 on v0

--- a/solution.py
+++ b/solution.py
@@ -1,7 +1,9 @@
+import functools
 import jax
 import jax.numpy as jnp
 from jax import lax
 from jax.sharding import PartitionSpec as P
+from jax.lax import axis_index, axis_size, ppermute
 
 HEAD_DIM = 72
 SEQ = 1024
@@ -11,6 +13,33 @@
 epsilon = 1e-06
 
 
+def apply_the_field(matrix, axis_name, ndim_at):
+    last = axis_size(axis_name)
+    then = axis_index(axis_name)
+    e_next, new, z1 = (last, then, matrix.shape[ndim_at])
+    u1 = jnp.zeros(
+        [k * e_next if h == ndim_at else k for h, k in enumerate(matrix.shape)], matrix.dtype
+    )
+    formed = lax.dynamic_update_slice_in_dim(u1, matrix, new * z1, axis=ndim_at)
+    y1 = r_now = matrix
+    for dev_j in range(1, e_next // 2 + 1):
+        y1 = ppermute(y1, axis_name, perm=[(h, (h + 1) % e_next) for h in range(e_next)])
+        formed = lax.dynamic_update_slice_in_dim(
+            formed, y1, (new - dev_j) % e_next * z1, axis=ndim_at
+        )
+        if 2 * dev_j < e_next:
+            r_now = ppermute(
+                r_now, axis_name=axis_name, perm=[(h, (h - 1) % e_next) for h in range(e_next)]
+            )
+            formed = lax.dynamic_update_slice_in_dim(
+                formed, r_now, (new + dev_j) % e_next * z1, axis=ndim_at
+            )
+    return formed
+
+
+unite_panels = functools.partial(apply_the_field, axis_name="dp", ndim_at=0)
+
+
 def normalize(values):
     centre = values - jnp.mean(values, axis=-1, keepdims=True)
     inverse = lax.rsqrt(jnp.mean(centre * centre, axis=-1, keepdims=True) + epsilon)
@@ -36,7 +65,7 @@
     columns = (
         lax.all_gather(w_qkv, "dp", axis=0, tiled=True),
         lax.all_gather(w_fc1, "dp", axis=0, tiled=True),
-        lax.all_gather(w_ada, "dp", axis=0, tiled=True),
+        unite_panels(w_ada),
     )
     row_parts = (
         lax.all_gather(w_proj, "dp", axis=1, tiled=True),

time: 1590 us -> 1550 us (0.975)
  waiting for transfers between devices: 1080 us -> 981 us
  starting transfers between devices: 2.35 us -> 47 us
    ppermute x0 -> x14, waiting for transfers between devices: none -> 142 us  [the longest x8 118 us: apply_the_field(): ppermute(y1, axis_name, perm=[(h, (h + 1) % e_next) for h in range(e_next)])]
    all_gather x2 -> x0, waiting for transfers between devices: 123 us -> none  [fetch_weights(): lax.all_gather(w_ada, 'dp', axis=0, tiled=True)]
    reduce_scatter x1, waiting for transfers between devices: 54.5 us -> 0.01 us  [shards(): lax.psum_scatter(grad_fc2, 'dp', scatter_dimension=1, tiled=True)]
    ppermute x0 -> x14, starting transfers between devices: none -> 44.7 us  [the longest x6 32.9 us: apply_the_field(): ppermute(r_now, axis_name=axis_name, perm=[(h, (h - 1) % e_next) for h in...]
    all_gather x2, waiting for transfers between devices: 77.4 us -> 40.8 us  [gather_rows(): return lax.all_gather(values, 'tensor', axis=0, tiled=True)]
    reduce_scatter x1, waiting for transfers between devices: 108 us -> 85.4 us  [shards(): lax.psum_scatter(grad_fc1, 'dp', scatter_dimension=0, tiled=True)]
  transfers between devices with their start and end apart: 22 -> 34, of which waited for: 20 -> 27; matrix products, arithmetic and copies ran while one was open for 14% -> 15% of each run, Pallas kernels for 0% -> 0%
where the time goes in v1:
time: 1550 us
  waiting for transfers between devices  981 us (63%)
  matrix products  225 us (15%)
  blocking collectives  126 us (8%)
  local copies, waits for them, and re-layouts  77.6 us (5%)
  other arithmetic  72.9 us (5%)
  starting transfers between devices  47 us (3%)
    reduce_scatter x1, waiting for transfers between devices, shards(): lax.psum_scatter(grad_ada, 'dp', scatter_dimension=0, tiled=True)  151 us
    ppermute x8, waiting for transfers between devices, apply_the_field(): ppermute(y1, axis_name, perm=[(h, (h + 1) % e_next) for h in range(e_next)])  118 us
    reduce_scatter x1, waiting for transfers between devices, shards(): lax.psum_scatter(grad_wqkv, 'dp', scatter_dimension=0, tiled=True)  90.7 us
    all_gather x2, waiting for transfers between devices, fetch_weights(): lax.all_gather(w_fc2, 'dp', axis=1, tiled=True)  90.3 us
    all_gather x2, waiting for transfers between devices, fetch_weights(): lax.all_gather(w_fc1, 'dp', axis=0, tiled=True)  86.5 us
    reduce_scatter x1, waiting for transfers between devices, shards(): lax.psum_scatter(grad_fc1, 'dp', scatter_dimension=0, tiled=True)  85.4 us
    reduce_scatter x2, waiting for transfers between devices, sum_back(): lax.psum_scatter(row_term(jnp.int32(0), lax.axis_size('tensor') * row_cou...  83.4 us
    reduce_scatter x1, waiting for transfers between devices, shards(): lax.psum_scatter(grad_proj, 'dp', scatter_dimension=1, tiled=True)  70.4 us
  transfers between devices with their start and end apart: 34, of which 27 were waited for; matrix products, arithmetic and copies ran while one was open for 15% of the time, Pallas kernels for 0%

profile of v1, /device:TPU:0, one launch (start us, length us, event | category | flops | bytes accessed | tf_op | source)
XLA Modules:
  0.0 1545.4 jit_solution(14119779915899425024)
XLA Ops:
  18.0 17.4 %collective-permute-done = bf16[144,1728]{1,0:T(8,128)(2,1)S(1)} collective-permute-done((bf16[144,1728]{1,0:T(8,128)(2,1)}, bf16[144,1728]{1,0:T(8,128)(2,1)S(1)}, u32[]{:S(2)}, u32[]{:S(2)}) %collective-permute-start) | collective-permute-done | bytes 497696 | tf_op jit(solution)/shard_map/ppermute | solution.py:26
  41.6 29.5 %collective-permute-done.2 = bf16[144,1728]{1,0:T(8,128)(2,1)S(1)} collective-permute-done((bf16[144,1728]{1,0:T(8,128)(2,1)S(1)}, bf16[144,1728]{1,0:T(8,128)(2,1)S(1)}, u32[]{:S(2)}, u32[]{:S(2)}) %collective-permute-start.2) | collective-permute-done | bytes 497696 | tf_op jit(solution)/shard_map/ppermute | solution.py:26
  128.5 35.4 %all_gather.42 = bf16[288,1152]{0,1:T(8,128)(2,1)} all-gather(bf16[288,144]{0,1:T(8,128)(2,1)S(1)} %copy-done.27), channel_id=1, replica_groups=mesh['dp'=8,'tensor'=4] {'dp'}, dimensions={1}, use_global_device_ids=true | all-gather | bytes 746496 | tf_op jit(solution)/shard_map/all_gather | solution.py:71
  196.1 51.5 %while.22 = (s32[]{:T(128)}, bf16[2,1024,4,72]{1,3,2,0:T(8,128)(2,1)}, f32[2,4,1024]{2,1,0:T(4,128)}, bf16[2,1024,4,72]{1,3,2,0:T(8,128)(2,1)}, bf16[2,1024,4,72...) while((s32[]{:T(128)}, bf16[2,1024,4,72]{1,3,2,0:T(8,128)(2,1)}, ...), condition=%wide.region_5.6_spmd, body=%wide.region_2.5_spmd.sunk | while | flops 1245999104 | bytes 66980012 | solution.py:207
  256.9 47.1 %reduce-scatter.13.cloned.1.call-done = bf16[512,1152]{1,0:T(8,128)(2,1)} async-done(((bf16[2048,1152]{1,0:T(8,128)(2,1)}), bf16[512,1152]{1,0:T(8,128)(2,1)}) %reduce-scatter.13.cloned.1.call-update) | async-done | bytes 1179664 | tf_op jit(solution)/shard_map/reduce_scatter | solution.py:209
  316.3 45.0 %all-gather.18.cloned.1.call-done = bf16[1152,1152]{1,0:T(8,128)(2,1)} async-done(((bf16[144,1152]{1,0:T(8,128)(2,1)}), bf16[1152,1152]{1,0:T(8,128)(2,1)}) %all-gather.18.cloned.1.call-update) | async-done | bytes 2654224 | tf_op jit(solution)/shard_map/all_gather | solution.py:67
  361.3 38.1 %all-gather.16.cloned.1.call-done = bf16[2048,1152]{1,0:T(8,128)(2,1)} async-done(((bf16[512,1152]{1,0:T(8,128)(2,1)}), bf16[2048,1152]{1,0:T(8,128)(2,1)}) %all-gather.16.cloned.1.call-update) | async-done | bytes 4718608 | tf_op jit(solution)/shard_map/all_gather | solution.py:78
  411.0 45.7 %all-gather.24.cloned.1.call-done = bf16[1152,1152]{0,1:T(8,128)(2,1)} async-done(((bf16[1152,144]{0,1:T(8,128)(2,1)}), bf16[1152,1152]{0,1:T(8,128)(2,1)}) %all-gather.24.cloned.1.call-update) | async-done | bytes 2654224 | tf_op jit(solution)/shard_map/all_gather | solution.py:72
  456.7 38.3 %all-gather.22.cloned.1.call-done = bf16[2048,1152]{1,0:T(8,128)(2,1)} async-done(((bf16[512,1152]{1,0:T(8,128)(2,1)}), bf16[2048,1152]{1,0:T(8,128)(2,1)}) %all-gather.22.cloned.1.call-update) | async-done | bytes 4718608 | tf_op jit(solution)/shard_map/all_gather | solution.py:239
  511.0 41.5 %all-gather.26.cloned.1.call-done = bf16[1152,1152]{1,0:T(8,128)(2,1)} async-done(((bf16[144,1152]{1,0:T(8,128)(2,1)}), bf16[1152,1152]{1,0:T(8,128)(2,1)}) %all-gather.26.cloned.1.call-update) | async-done | bytes 2654224 | tf_op jit(solution)/shard_map/all_gather | solution.py:67
  564.0 44.6 %all-gather.20.cloned.1.call-done = bf16[1152,1152]{0,1:T(8,128)(2,1)} async-done(((bf16[1152,144]{0,1:T(8,128)(2,1)}), bf16[1152,1152]{0,1:T(8,128)(2,1)}) %all-gather.20.cloned.1.call-update) | async-done | bytes 2654224 | tf_op jit(solution)/shard_map/all_gather | solution.py:72
  622.3 35.3 %reduce-scatter.17.cloned.1.call-done = bf16[512,1152]{1,0:T(8,128)(2,1)} async-done(((bf16[2048,1152]{1,0:T(8,128)(2,1)}), bf16[512,1152]{1,0:T(8,128)(2,1)}) %reduce-scatter.17.cloned.1.call-update) | async-done | bytes 1179664 | tf_op jit(solution)/shard_map/reduce_scatter | solution.py:82
  661.1 46.9 %reduce-scatter.15.cloned.1.call-done = bf16[512,1152]{1,0:T(8,128)(2,1)} async-done(((bf16[2048,1152]{1,0:T(8,128)(2,1)}), bf16[512,1152]{1,0:T(8,128)(2,1)}) %reduce-scatter.15.cloned.1.call-update) | async-done | bytes 1179664 | tf_op jit(solution)/shard_map/reduce_scatter | solution.py:224
  715.9 32.4 %all_gather.50 = bf16[288,1152]{0,1:T(8,128)(2,1)S(1)} all-gather(bf16[288,144]{0,1:T(8,128)(2,1)S(1)} %copy-done.28), channel_id=1, replica_groups=mesh['dp'=8,'tensor'=4] {'dp'}, dimensions={1}, use_global_device_ids=true | all-gather | bytes 746496 | tf_op jit(solution)/shard_map/all_gather | solution.py:71
  765.4 75.8 %while.23 = (s32[]{:T(128)}, bf16[2,1024,4,3,72]{1,4,2,3,0:T(8,128)(2,1)}, bf16[2,1024,4,72]{1,3,2,0:T(8,128)(2,1)S(1)}, bf16[2,1024,4,72]{1,3,2,0:T(8,128)(2,1)...) while((s32[]{:T(128)}, ...), condition=%wide.region_15.16_spmd, body=%wide.region_13.15_spmd.sunk | while | flops 3077009408 | bytes 199608528 | solution.py:254
  858.3 48.1 %reduce-scatter.19.cloned.1.call-done = bf16[512,1152]{1,0:T(8,128)(2,1)} async-done(((bf16[2048,1152]{1,0:T(8,128)(2,1)}), bf16[512,1152]{1,0:T(8,128)(2,1)}) %reduce-scatter.19.cloned.1.call-update) | async-done | bytes 1179664 | tf_op jit(solution)/shard_map/reduce_scatter | solution.py:82
  981.6 23.3 %collective-permute-done.7 = bf16[144,1728]{1,0:T(8,128)(2,1)S(1)} collective-permute-done((bf16[144,1728]{1,0:T(8,128)(2,1)S(1)}, bf16[144,1728]{1,0:T(8,128)(2,1)S(1)}, u32[]{:S(2)}, u32[]{:S(2)}) %collective-permute-start.7) | collective-permute-done | bytes 497696 | tf_op jit(solution)/shard_map/ppermute | solution.py:26
  1014.8 19.4 %collective-permute-done.9 = bf16[144,1728]{1,0:T(8,128)(2,1)S(1)} collective-permute-done((bf16[144,1728]{1,0:T(8,128)(2,1)S(1)}, bf16[144,1728]{1,0:T(8,128)(2,1)S(1)}, u32[]{:S(2)}, u32[]{:S(2)}) %collective-permute-start.9) | collective-permute-done | bytes 497696 | tf_op jit(solution)/shard_map/ppermute | solution.py:26
  1037.9 20.4 %collective-permute-start.12 = (bf16[144,1728]{1,0:T(8,128)(2,1)S(1)}, bf16[144,1728]{1,0:T(8,128)(2,1)S(1)}, u32[]{:S(2)}, u32[]{:S(2)}) collective-permute-start(bf16[144,1728]{1,0:T(8,128)(2,1)S(1)} %collective-permute-done.10), channel_id=1, source_target_pairs={{0,28},{4,0},{8,4},{12,8},{16,12},{20,16},{24,20},{28,24},{1,29},{... | collective-permute-start | bytes 1493000 | tf_op jit(solution)/shard_map/ppermute | solution.py:31
  1099.1 41.5 %all-reduce = (f32[1728]{0:T(1024)}, f32[576]{0:T(1024)}, f32[1152]{0:T(1024)}, f32[1152]{0:T(1024)}, f32[1152]{0:T(1024)}) all-reduce(f32[1728]{0:T(1024)S(1)} %convert_reduce_fusion.5, f32[576]{0:T(1024)S(1)} %reshape.219, f32[1152]{0:T(1024)S(1)} %get-tuple-element.178, ...), channel_id=1, replica_groups=mesh['dp'=8,'tensor'=4] {'dp'}, use_global_device_ids=true, to_apply=%region_23.24 | all-reduce | flops 5760 | bytes 46080 | tf_op jit(solution)/shard_map/psum | solution.py:286
  1140.7 85.4 %reduce-scatter.27.cloned.1.call-done = f32[144,1152]{1,0:T(8,128)} async-done(((f32[1152,1152]{1,0:T(8,128)}), f32[144,1152]{1,0:T(8,128)}) %reduce-scatter.27.cloned.1.call-update) | async-done | bytes 663568 | tf_op jit(solution)/shard_map/reduce_scatter | solution.py:291
  1226.1 70.4 %reduce-scatter.25.cloned.1.call-done = f32[288,144]{0,1:T(8,128)} async-done(((f32[288,1152]{0,1:T(8,128)}), f32[288,144]{0,1:T(8,128)}) %reduce-scatter.25.cloned.1.call-update) | async-done | bytes 165904 | tf_op jit(solution)/shard_map/reduce_scatter | solution.py:295
  1296.5 90.7 %reduce-scatter.23.cloned.1.call-done = f32[144,864]{1,0:T(8,128)} async-done(((f32[1152,864]{1,0:T(8,128)}), f32[144,864]{1,0:T(8,128)}) %reduce-scatter.23.cloned.1.call-update) | async-done | bytes 497680 | tf_op jit(solution)/shard_map/reduce_scatter | solution.py:290
  1387.2 151.2 %reduce-scatter.21.cloned.1.call-done = f32[144,1728]{1,0:T(8,128)} async-done(((f32[1152,1728]{1,0:T(8,128)}), f32[144,1728]{1,0:T(8,128)}) %reduce-scatter.21.cloned.1.call-update) | async-done | bytes 995344 | tf_op jit(solution)/shard_map/reduce_scatter | solution.py:292
  (310 shorter events, 481.9 us)
Async XLA Ops:
  7.2 156.7 %all-gather.14.cloned.1.call-start = ((), (), s32[]{:S(2)}) async-start(), calls=%async_computation.11 | async-start | bytes 2322432 | tf_op jit(solution)/shard_map/all_gather | solution.py:66
  13.4 153.2 %all-gather.12.cloned.1.call-start = ((), (), s32[]{:S(2)}) async-start(), calls=%async_computation.10 | async-start | bytes 5898240 | tf_op jit(solution)/shard_map/all_gather | solution.py:78
  35.4 35.7 %collective-permute-start.2 = (bf16[144,1728]{1,0:T(8,128)(2,1)S(1)}, bf16[144,1728]{1,0:T(8,128)(2,1)S(1)}, u32[]{:S(2)}, u32[]{:S(2)}) collective-permute-start(bf16[144,1728]{1,0:T(8,128)(2,1)S(1)} %collective-permute-done), channel_id=1, source_target_pairs={{0,4},{4,8},{8,12},{12,16},{16,20},{20,24},{24,28},{28,0},{1,5},{5... | collective-permute-start | bytes 1493000 | tf_op jit(solution)/shard_map/ppermute | solution.py:26
  38.2 42.3 %collective-permute-start.3 = (bf16[144,1728]{1,0:T(8,128)(2,1)S(1)}, bf16[144,1728]{1,0:T(8,128)(2,1)S(1)}, u32[]{:S(2)}, u32[]{:S(2)}) collective-permute-start(bf16[144,1728]{1,0:T(8,128)(2,1)S(1)} %collective-permute-done.1), channel_id=1, source_target_pairs={{0,28},{4,0},{8,4},{12,8},{16,12},{20,16},{24,20},{28,24},{1,29},{... | collective-permute-start | bytes 1493000 | tf_op jit(solution)/shard_map/ppermute | solution.py:31
  128.3 175.7 %reduce-scatter.13.cloned.1.call-start = ((), (), s32[]{:S(2)}) async-start(), calls=%async_computation.12 | async-start | bytes 5898240 | tf_op jit(solution)/shard_map/reduce_scatter | solution.py:209
  256.0 105.3 %all-gather.18.cloned.1.call-start = ((), (), s32[]{:S(2)}) async-start(), calls=%async_computation.14 | async-start | bytes 2985984 | tf_op jit(solution)/shard_map/all_gather | solution.py:67
  256.6 142.9 %all-gather.16.cloned.1.call-start = ((), (), s32[]{:S(2)}) async-start(), calls=%async_computation.13 | async-start | bytes 5898240 | tf_op jit(solution)/shard_map/all_gather | solution.py:78
  313.4 143.3 %all-gather.24.cloned.1.call-start = ((), (), s32[]{:S(2)}) async-start(), calls=%async_computation.18 | async-start | bytes 2985984 | tf_op jit(solution)/shard_map/all_gather | solution.py:72
  314.0 181.0 %all-gather.22.cloned.1.call-start = ((), (), s32[]{:S(2)}) async-start(), calls=%async_computation.17 | async-start | bytes 5898240 | tf_op jit(solution)/shard_map/all_gather | solution.py:239
  314.8 237.7 %all-gather.26.cloned.1.call-start = ((), (), s32[]{:S(2)}) async-start(), calls=%async_computation.19 | async-start | bytes 2985984 | tf_op jit(solution)/shard_map/all_gather | solution.py:67
  315.5 293.0 %all-gather.20.cloned.1.call-start = ((), (), s32[]{:S(2)}) async-start(), calls=%async_computation.15 | async-start | bytes 2985984 | tf_op jit(solution)/shard_map/all_gather | solution.py:72
  316.3 341.3 %reduce-scatter.17.cloned.1.call-start = ((), (), s32[]{:S(2)}) async-start(), calls=%async_computation.20 | async-start | bytes 5898240 | tf_op jit(solution)/shard_map/reduce_scatter | solution.py:82
  563.5 144.4 %reduce-scatter.15.cloned.1.call-start = ((), (), s32[]{:S(2)}) async-start(), calls=%async_computation.16 | async-start | bytes 5898240 | tf_op jit(solution)/shard_map/reduce_scatter | solution.py:224
  621.6 131.9 %all-gather.28.cloned.1.call-start = ((), (), s32[]{:S(2)}) async-start(), calls=%async_computation.21 | async-start | bytes 5898240 | tf_op jit(solution)/shard_map/all_gather | solution.py:251
  715.8 132.2 %all-gather.30.cloned.1.call-start = ((), (), s32[]{:S(2)}) async-start(), calls=%async_computation.22 | async-start | bytes 2322432 | tf_op jit(solution)/shard_map/all_gather | solution.py:66
  748.4 158.0 %reduce-scatter.19.cloned.1.call-start = ((), (), s32[]{:S(2)}) async-start(), calls=%async_computation.23 | async-start | bytes 5898240 | tf_op jit(solution)/shard_map/reduce_scatter | solution.py:82
  858.2 111.5 %reduce-scatter.31.cloned.1.call-start = ((), (), s32[]{:S(2)}) async-start(), calls=%async_computation.29 | async-start | bytes 2211840
  925.4 215.2 %reduce-scatter.29.cloned.1.call-start = ((), (), s32[]{:S(2)}) async-start(), calls=%async_computation.28 | async-start | bytes 5971968 | tf_op jit(solution)/shard_map/reduce_scatter | solution.py:296
  940.0 286.1 %reduce-scatter.27.cloned.1.call-start = ((), (), s32[]{:S(2)}) async-start(), calls=%async_computation.27 | async-start | bytes 5971968 | tf_op jit(solution)/shard_map/reduce_scatter | solution.py:291
  953.0 343.5 %reduce-scatter.25.cloned.1.call-start = ((), (), s32[]{:S(2)}) async-start(), calls=%async_computation.26 | async-start | bytes 1990656 | tf_op jit(solution)/shard_map/reduce_scatter | solution.py:295
  959.9 427.3 %reduce-scatter.23.cloned.1.call-start = ((), (), s32[]{:S(2)}) async-start(), calls=%async_computation.25 | async-start | bytes 4644864 | tf_op jit(solution)/shard_map/reduce_scatter | solution.py:290
  969.6 568.8 %reduce-scatter.21.cloned.1.call-start = ((), (), s32[]{:S(2)}) async-start(), calls=%async_computation.24 | async-start | bytes 9289728 | tf_op jit(solution)/shard_map/reduce_scatter | solution.py:292
  1034.1 32.7 %collective-permute-start.11 = (bf16[144,1728]{1,0:T(8,128)(2,1)S(1)}, bf16[144,1728]{1,0:T(8,128)(2,1)S(1)}, u32[]{:S(2)}, u32[]{:S(2)}) collective-permute-start(bf16[144,1728]{1,0:T(8,128)(2,1)S(1)} %collective-permute-done.9), channel_id=1, source_target_pairs={{0,4},{4,8},{8,12},{12,16},{16,20},{20,24},{24,28},{28,0},{1,5},{5... | collective-permute-start | bytes 1493000 | tf_op jit(solution)/shard_map/ppermute | solution.py:26
  1037.9 33.2 %collective-permute-start.12 = (bf16[144,1728]{1,0:T(8,128)(2,1)S(1)}, bf16[144,1728]{1,0:T(8,128)(2,1)S(1)}, u32[]{:S(2)}, u32[]{:S(2)}) collective-permute-start(bf16[144,1728]{1,0:T(8,128)(2,1)S(1)} %collective-permute-done.10), channel_id=1, source_target_pairs={{0,28},{4,0},{8,4},{12,8},{16,12},{20,16},{24,20},{28,24},{1,29},{... | collective-permute-start | bytes 1493000 | tf_op jit(solution)/shard_map/ppermute | solution.py:31
  (71 other events, 2010.2 us)
Sparse Core Ops, SparseCore 0:
  13.5 79.1 all-gather.13
  128.4 38.0 all-gather.11
  256.1 47.8 reduce-scatter.12
  306.2 55.0 all-gather.17
  363.4 36.0 all-gather.15
  401.7 55.0 all-gather.23
  459.0 36.0 all-gather.21
  497.4 55.0 all-gather.25
  554.9 53.5 all-gather.19
  611.1 46.4 reduce-scatter.16
  660.1 47.8 reduce-scatter.14
  716.0 37.4 all-gather.27
  755.9 48.9 all-gather.29
  858.3 47.9 reduce-scatter.18
  925.5 29.3 reduce-scatter.30
  959.4 158.5 reduce-scatter.28
  1122.0 103.9 reduce-scatter.26
  1230.4 66.0 reduce-scatter.24
  1300.6 86.5 reduce-scatter.22
  1391.7 146.5 reduce-scatter.20
